TPU v7x, 32 devices: a whole 2x2x4 slice. The times are simulated.
32 devices in a mesh: mp: 2 (over core), feat: 16 (over z, y, x).
Axes of the slice: x: 2, y: 2, z: 4, core: 2. Of those that a mesh axis runs over, the one named last changes fastest.
Arguments:
- residual: bfloat16 [2, 96, 2304], P(None, 'feat', 'mp'), may hold values from -6 to 6
- norm_gain: float32 [2, 2304], P(None, 'mp'), may hold values from 0.1 to 1.9
- gate_weight: bfloat16 [2, 2304, 9216], P(None, 'mp', 'feat'), may hold values from -0.125 to 0.125
- up_weight: bfloat16 [2, 2304, 9216], P(None, 'mp', 'feat'), may hold values from -0.125 to 0.125
- down_weight: bfloat16 [2, 9216, 2304], P(None, 'feat', 'mp'), may hold values from -0.0625 to 0.0625
- encoder: bfloat16 [2, 32768, 2304], P(None, 'feat', 'mp'), may hold values from -0.125 to 0.125
- encoder_bias: float32 [2, 32768], P(None, 'feat'), may hold values from -3 to 3
- decoder: bfloat16 [3, 32768, 2304], P(None, 'feat', 'mp'), may hold values from -0.03125 to 0.03125
Outputs:
- grad_encoder: bfloat16 [2, 32768, 2304], P(None, 'feat', 'mp')
- grad_bias: float32 [2, 32768], P(None, 'feat')
- grad_decoder: bfloat16 [3, 32768, 2304], P(None, 'feat', 'mp')
All inputs are finite; a program needn't handle non-finite values.
Results may differ from a plain program's by a relative error of at most 0.02.
The roundings to bfloat16 on the way count: a program that leaves them out, or rounds other values in their place, can miss the bound.
Values may be sent and summed in bfloat16 or wider, within the bound.
No kernel may reach another device: no remote copies, remote signals or barrier semaphores. Data moves between devices by JAX's collectives and lax.ppermute only.
A program may use at most 128 MiB of HBM per device.

v0:
```python
import math
import jax
import jax.numpy as jnp
from jax import lax
from jax.sharding import PartitionSpec as P

D = 2304
sparsity_weight = 0.1


def outer_product(weights_side, errors_side):
    return lax.dot_general(
        weights_side, errors_side, (((0,), (0,)), ((), ())), preferred_element_type=jnp.float32
    )


def body(residual, norm_gain, gate_weight, up_weight, down_weight, encoder, encoder_bias, decoder):
    values = residual.astype(jnp.float32)
    squares = lax.psum(jnp.sum(values * values, axis=2), "mp")
    inverse_rms = lax.rsqrt(squares / D + 1e-06)
    normed_local = (values * inverse_rms[:, :, None] * norm_gain[:, None, :]).astype(jnp.bfloat16)
    normed = lax.all_gather(normed_local, "feat", axis=1, tiled=True)
    tokens = normed.shape[1]
    local_rows = residual.shape[1]
    gate_part = jnp.einsum("ltd,ldh->lth", normed, gate_weight, preferred_element_type=jnp.float32)
    up_part = jnp.einsum("ltd,ldh->lth", normed, up_weight, preferred_element_type=jnp.float32)
    gate_part, up_part = (
        lax.psum(gate_part.astype(jnp.bfloat16), "mp").astype(jnp.float32),
        lax.psum(up_part.astype(jnp.bfloat16), "mp").astype(jnp.float32),
    )
    hidden = (jax.nn.gelu(gate_part, approximate=True) * up_part).astype(jnp.bfloat16)
    preact_part = jnp.einsum("ltd,lfd->tlf", normed, encoder, preferred_element_type=jnp.float32)
    preact = lax.psum(preact_part, "mp")
    active = jnp.maximum(preact + encoder_bias[None], 0.0).astype(jnp.bfloat16)
    features = active.shape[2]
    model_cols = decoder.shape[2]
    joined = jnp.concatenate([decoder[1], decoder[2]], axis=0)
    picked = hidden
    partial_value = jnp.einsum(
        "lth,lhd->tld", picked, down_weight, preferred_element_type=jnp.float32
    )
    picked = active
    first_part = jnp.dot(picked[:, 0], decoder[0], preferred_element_type=jnp.float32)
    second = jnp.dot(
        picked.reshape(local_rows * lax.axis_size("feat"), 2 * features),
        joined,
        preferred_element_type=jnp.float32,
    )
    errors_local = lax.psum_scatter(
        jnp.concatenate([first_part, second], axis=1)
        - partial_value.reshape(local_rows * lax.axis_size("feat"), -1),
        "feat",
        scatter_dimension=0,
        tiled=True,
    ).astype(jnp.bfloat16)
    errors = lax.all_gather(errors_local, "feat", axis=0, tiled=True)
    error_first = errors[:, :model_cols]
    error_second = errors[:, model_cols:]
    first_rows = jnp.concatenate([decoder[0], decoder[1]], axis=1)
    back_first = lax.dot_general(
        errors, first_rows, (((1,), (1,)), ((), ())), preferred_element_type=jnp.float32
    )
    back_second = lax.dot_general(
        error_second, decoder[2], (((1,), (1,)), ((), ())), preferred_element_type=jnp.float32
    )
    back_stack = jnp.stack([back_first, back_second], axis=1)
    loss_scale = 1.0 / math.sqrt(tokens)
    backward = lax.psum(back_stack.astype(jnp.bfloat16), "mp").astype(jnp.float32)
    pre_grad = jnp.where(active > 0, loss_scale * (backward + sparsity_weight), 0.0).astype(
        jnp.bfloat16
    )
    grad_encoder = jnp.einsum(
        "tlf,ltd->lfd", pre_grad, normed, preferred_element_type=jnp.float32
    ).astype(jnp.bfloat16)
    grad_bias = jnp.sum(pre_grad.astype(jnp.float32), axis=0)
    active_first = active[:, 0]
    active_second = active[:, 1]
    grad_decoder = (
        loss_scale
        * jnp.stack(
            [
                outer_product(active_first, error_first),
                outer_product(active_first, error_second),
                outer_product(active_second, error_second),
            ]
        )
    ).astype(jnp.bfloat16)
    return (grad_encoder, grad_bias, grad_decoder)


def solution(mesh):
    return jax.shard_map(
        body,
        mesh=mesh,
        in_specs=(
            P(None, "feat", "mp"),
            P(None, "mp"),
            P(None, "mp", "feat"),
            P(None, "mp", "feat"),
            P(None, "feat", "mp"),
            P(None, "feat", "mp"),
            P(None, "feat"),
            P(None, "feat", "mp"),
        ),
        out_specs=(P(None, "feat", "mp"), P(None, "feat"), P(None, "feat", "mp")),
        check_vma=False,
    )
```

profile of v0, /device:TPU:0, one launch (start us, length us, event | category | flops | bytes accessed | tf_op | source)
XLA Modules:
  0.0 270.2 jit_solution(11253927287694514613)
XLA Ops:
  7.2 1.0 fusion.38
  8.2 2.6 psum.35
  10.9 0.8 fusion.40
  11.7 44.8 %all_gather.6 = bf16[2,96,1152]{2,0,1:T(2,128)(2,1)S(1)} all-gather(bf16[2,6,1152]{2,0,1:T(2,128)(2,1)S(1)} %fusion.40), channel_id=1, replica_groups=mesh['mp'=2,'feat'=16] {'feat'}, dimensions={1}, use_global_device_ids=true | all-gather | bytes 470016 | tf_op jit(solution)/shard_map/all_gather | solution.py:22
  56.5 3.6 %convolution_convert_fusion.3 = bf16[2,96,576]{2,1,0:T(8,128)(2,1)} fusion(bf16[2,1152,576]{1,2,0:T(8,128)(2,1)} %param.10, bf16[2,96,1152]{2,0,1:T(2,128)(2,1)S(1)} %all_gather.6), kind=kOutput, calls=%fused_computation.27 | convolution fusion | flops 254914560 | bytes 3317760 | tf_op jit(solution)/shard_map/ltd,ldh->lth/dot_general | solution.py:25
  60.1 3.4 %convolution_convert_fusion.2 = bf16[2,96,576]{2,1,0:T(8,128)(2,1)} fusion(bf16[2,1152,576]{1,2,0:T(8,128)(2,1)} %param.11, bf16[2,96,1152]{2,0,1:T(2,128)(2,1)S(1)} %all_gather.6), kind=kOutput, calls=%fused_computation.26 | convolution fusion | flops 254914560 | bytes 3317760 | tf_op jit(solution)/shard_map/ltd,ldh->lth/dot_general | solution.py:26
  63.6 8.0 %convolution_bitcast_fusion.4 = f32[96,2,2048]{2,0,1:T(8,128)} fusion(bf16[2,2048,1152]{2,1,0:T(8,128)(2,1)} %param.13, bf16[2,96,1152]{2,0,1:T(2,128)(2,1)S(1)} %all_gather.6), kind=kOutput, calls=%fused_computation.18 | convolution fusion | flops 905969664 | bytes 11452416 | tf_op jit(solution)/shard_map/ltd,lfd->tlf/dot_general | solution.py:32
  71.7 11.3 %slice_bitcast_fusion.2 = (bf16[2048,1152]{1,0:T(8,128)(2,1)}, bf16[2048,1152]{1,0:T(8,128)(2,1)}, bf16[2048,1152]{1,0:T(8,128)(2,1)}) fusion(bf16[3,2048,1152]{2,1,0:T(8,128)(2,1)} %param.15), kind=kLoop, calls=%fused_computation.16 | loop fusion | bytes 28311552 | tf_op jit(solution)/shard_map/squeeze | solution.py:43
  83.0 1.7 convolution_bitcast_fusion.3
  84.8 17.4 %all-reduce.7.cloned.1.call-done = f32[96,2,2048]{2,0,1:T(8,128)} async-done(((f32[96,2,2048]{2,0,1:T(8,128)}), f32[96,2,2048]{2,0,1:T(8,128)}) %all-reduce.7.cloned.1.call-update) | async-done | bytes 1572880 | tf_op jit(solution)/shard_map/psum | solution.py:33
  102.1 1.7 maximum_convert_fusion
  103.9 3.7 %fusion.24 = f32[96,1152]{1,0:T(8,128)S(1)} fusion(bf16[96,2,2048]{2,0,1:T(8,128)(2,1)S(1)} %maximum_convert_fusion, bf16[3,2048,1152]{2,1,0:T(8,128)(2,1)} %param.15), kind=kOutput, calls=%fused_computation.43 | convolution fusion | flops 452984832 | bytes 5554176 | tf_op jit(solution)/shard_map/dot_general | solution.py:43
  107.9 0.6 copy-done.4
  108.5 2.0 fusion.2
  110.6 49.0 %fusion = f32[8,2304]{1,0:T(8,128)S(1)} fusion(f32[96,2304]{1,0:T(8,128)S(1)} %maximum_subtract_fusion), kind=kCustom, calls=%all-reduce-scatter | all-reduce-scatter fusion | flops 294913 | bytes 958976
  159.6 1.3 collective-permute-start.1
  160.9 1.3 collective-permute-start.2
  162.2 1.9 collective-permute-start
  164.1 2.4 collective-permute-start.3
  166.5 0.6 dynamic-slice.4
  167.8 0.4 collective-permute-done.3
  168.1 0.6 concatenate.12
  168.8 43.6 %all-gather = bf16[16,6,2304]{2,1,0:T(8,128)(2,1)S(1)} all-gather(bf16[1,6,2304]{2,1,0:T(8,128)(2,1)S(1)} %fusion.41), channel_id=1, replica_groups=mesh['mp'=2,'feat'=16] {'feat'}, dimensions={0}, use_global_device_ids=true | all-gather | bytes 470016 | tf_op jit(solution)/shard_map/all_gather | solution.py:56
  212.5 3.9 %fusion.16 = bf16[96,1,2048]{2,0,1:T(8,128)(2,1)S(1)} fusion(bf16[96,2304]{1,0:T(8,128)(2,1)S(1)} %reshape.18, bf16[3,2048,1152]{2,1,0:T(8,128)(2,1)} %param.15), kind=kOutput, calls=%fused_computation.22 | convolution fusion | flops 453181440 | bytes 5332992 | tf_op jit(solution)/shard_map/dot_general | solution.py:63
  216.4 5.1 %convolution_bitcast_fusion.1 = f32[1,2048,1152]{2,1,0:T(8,128)} fusion(bf16[96,2,2048]{2,0,1:T(8,128)(2,1)S(1)} %maximum_convert_fusion, bf16[96,2304]{1,0:T(8,128)(2,1)S(1)} %reshape.18), kind=kOutput, calls=%fused_computation.12 | convolution fusion | flops 452984832 | bytes 10051584 | tf_op jit(solution)/shard_map/dot_general | solution.py:12
  221.5 5.8 %convolution_bitcast_fusion = f32[1,2048,1152]{2,1,0:T(8,128)} fusion(bf16[96,2,2048]{2,0,1:T(8,128)(2,1)S(1)} %maximum_convert_fusion, bf16[96,2304]{1,0:T(8,128)(2,1)S(1)} %reshape.18), kind=kOutput, calls=%fused_computation.11 | convolution fusion | flops 452984832 | bytes 10051584 | tf_op jit(solution)/shard_map/dot_general | solution.py:12
  227.3 5.1 %convolution_bitcast_fusion.2 = f32[1,2048,1152]{2,1,0:T(8,128)} fusion(bf16[96,2,2048]{2,0,1:T(8,128)(2,1)S(1)} %maximum_convert_fusion, bf16[96,2304]{1,0:T(8,128)(2,1)S(1)} %reshape.18), kind=kOutput, calls=%fused_computation.13 | convolution fusion | flops 452984832 | bytes 10051584 | tf_op jit(solution)/shard_map/dot_general | solution.py:12
  232.4 3.1 %fusion.13 = bf16[96,1,2048]{2,0,1:T(8,128)(2,1)S(1)} fusion(bf16[96,2304]{1,0:T(8,128)(2,1)S(1)} %reshape.18, bf16[2048,1152]{1,0:T(8,128)(2,1)S(1)} %bitcast.51, bf16[2048,1152]{1,0:T(8,128)(2,1)S(1)} %bitcast.47), kind=kOutput, calls=%fused_computation.21 | convolution fusion | flops 925040640 | bytes 10272768 | tf_op jit(solution)/shard_map/dot_general | solution.py:60
  235.6 1.0 pad_maximum_fusion
  236.5 16.6 %fusion.1 = bf16[3,2048,1152]{2,1,0:T(8,128)(2,1)} fusion(f32[1,2048,1152]{2,1,0:T(8,128)} %convolution_bitcast_fusion, f32[1,2048,1152]{2,1,0:T(8,128)} %convolution_bitcast_fusion.1, f32[1,2048,1152]{2,1,0:T(8,128)} %convolution_bitcast_fusion.2), kind=kLoop, calls=%fused_computation.1 | loop fusion | flops 28311552 | bytes 42467328 | tf_op jit(solution)/shard_map/convert_element_type | solution.py:87
  253.2 2.8 %convert_reduce_fusion = f32[2,2048]{1,0:T(2,128)} fusion(bf16[96,2,2048]{2,0,1:T(8,128)(2,1)} %all-reduce.9.cloned.1.call-done, f32[96,2,2048]{2,0,1:T(8,128)} %all-reduce.7.cloned.1.call-done, f32[2,2048]{1,0:T(2,128)S(1)} %copy-done.5), kind=kLoop, calls=%fused_computation.23 | loop fusion | flops 4321280 | bytes 2392064 | tf_op jit(solution)/shard_map/reduce_sum | solution.py:75
  256.0 7.6 %convolution_convert_fusion = bf16[2,2048,1152]{2,1,0:T(8,128)(2,1)} fusion(bf16[2,96,1152]{2,0,1:T(2,128)(2,1)} %copy-done.3, bf16[96,2,2048]{2,0,1:T(8,128)(2,1)} %all-reduce.9.cloned.1.call-done, bf16[96,2,2048]{2,0,1:T(8,128)(2,1)S(1)} %maximum_convert_fusion), kind=kOutput, calls=%fused_computation.2 | convolution fusion | flops 913047552 | bytes 11452416 | tf_op jit(solution)/shard_map/tlf,ltd->lfd/dot_general | solution.py:72
  (48 shorter events, 0.9 us)
Async XLA Ops:
  7.2 75.8 %copy-start = (bf16[2,576,1152]{2,1,0:T(8,128)(2,1)S(1)}, bf16[2,576,1152]{2,1,0:T(8,128)(2,1)}, u32[]{:S(2)}) copy-start(bf16[2,576,1152]{2,1,0:T(8,128)(2,1)} %param.12) | copy-start | bytes 7962628
  7.2 75.8 %all-reduce.11.cloned.1.call-start = ((), (), s32[]{:S(2)}) async-start(), calls=%async_computation.2 | async-start | bytes 983040 | tf_op jit(solution)/shard_map/psum | solution.py:28
  56.5 15.0 %copy-start.3 = (bf16[2,96,1152]{2,0,1:T(2,128)(2,1)}, bf16[2,96,1152]{2,0,1:T(2,128)(2,1)S(1)}, u32[]{:S(2)}) copy-start(bf16[2,96,1152]{2,0,1:T(2,128)(2,1)S(1)} %all_gather.6) | copy-start | bytes 1327108
  63.5 38.6 %all-reduce.7.cloned.1.call-start = ((), (), s32[]{:S(2)}) async-start(), calls=%async_computation | async-start | bytes 3145728 | tf_op jit(solution)/shard_map/psum | solution.py:33
  71.6 181.6 %all-reduce.9.cloned.1.call-start = ((), (), s32[]{:S(2)}) async-start(), calls=%async_computation.1 | async-start | bytes 1572864 | tf_op jit(solution)/shard_map/psum | solution.py:68
  83.0 19.1 %copy-start.5 = (f32[2,2048]{1,0:T(2,128)S(1)}, f32[2,2048]{1,0:T(2,128)}, u32[]{:S(2)}) copy-start(f32[2,2048]{1,0:T(2,128)} %param.14) | copy-start | bytes 49156
  102.1 5.4 %copy-start.2 = (f32[96,2,2048]{2,0,1:T(8,128)S(1)}, f32[96,2,2048]{2,0,1:T(8,128)}, u32[]{:S(2)}) copy-start(f32[96,2,2048]{2,0,1:T(8,128)} %all-reduce.7.cloned.1.call-done) | copy-start | bytes 4718596
  102.1 5.7 %slice-start.2 = ((s8[4718592]{0:T(1024)(128)(4,1)}), s8[4194304]{0:T(1024)(128)(4,1)S(1)}, s32[]{:S(2)}) async-start(s8[4718592]{0:T(1024)(128)(4,1)} %bitcast.48), calls=%async_computation.5 | async-start | bytes 8388608
  103.9 4.0 %slice-start.3 = ((s8[4718592]{0:T(1024)(128)(4,1)}), s8[524288]{0:T(1024)(128)(4,1)S(1)}, s32[]{:S(2)}) async-start(s8[4718592]{0:T(1024)(128)(4,1)} %bitcast.48), calls=%async_computation.6 | async-start | bytes 1048576
  103.9 4.6 %copy-start.4 = (bf16[2048,1152]{1,0:T(8,128)(2,1)S(1)}, bf16[2048,1152]{1,0:T(8,128)(2,1)}, u32[]{:S(2)}) copy-start(bf16[2048,1152]{1,0:T(8,128)(2,1)} %get-tuple-element.6) | copy-start | bytes 14155780
  108.5 58.1 %copy-start.6 = (u32[32]{0:T(128)S(1)}, u32[32]{0:T(128)}, u32[]{:S(2)}) copy-start(u32[32]{0:T(128)} %constant.26) | copy-start | bytes 388
  159.6 8.5 %collective-permute-start.1 = (bf16[8,2304]{1,0:T(8,128)(2,1)S(1)}, bf16[8,2304]{1,0:T(8,128)(2,1)S(1)}, u32[]{:S(2)}, u32[]{:S(2)}) collective-permute-start(bf16[8,2304]{1,0:T(8,128)(2,1)S(1)} %convert.22), channel_id=1, source_target_pairs={{0,2},{1,3},{2,4},{3,5},{4,6},{5,7},{6,8},{7,9},{8,10},{9,11},{10,... | collective-permute-start | bytes 110600
  160.9 7.2 %collective-permute-start.2 = (bf16[8,2304]{1,0:T(8,128)(2,1)S(1)}, bf16[8,2304]{1,0:T(8,128)(2,1)S(1)}, u32[]{:S(2)}, u32[]{:S(2)}) collective-permute-start(bf16[8,2304]{1,0:T(8,128)(2,1)S(1)} %convert.22), channel_id=1, source_target_pairs={{0,3},{1,4},{2,5},{3,6},{4,7},{5,8},{6,9},{7,10},{8,11},{9,12},{10... | collective-permute-start | bytes 110600
  162.2 5.9 %collective-permute-start = (bf16[8,2304]{1,0:T(8,128)(2,1)S(1)}, bf16[8,2304]{1,0:T(8,128)(2,1)S(1)}, u32[]{:S(2)}, u32[]{:S(2)}) collective-permute-start(bf16[8,2304]{1,0:T(8,128)(2,1)S(1)} %convert.22), channel_id=1, source_target_pairs={{0,1},{1,2},{2,3},{3,4},{4,5},{5,6},{6,7},{7,8},{8,9},{9,10},{10,1... | collective-permute-start | bytes 110600
  164.1 4.0 %collective-permute-start.3 = (bf16[6,2304]{1,0:T(8,128)(2,1)S(1)}, bf16[6,2304]{1,0:T(8,128)(2,1)S(1)}, u32[]{:S(2)}, u32[]{:S(2)}) collective-permute-start(bf16[6,2304]{1,0:T(8,128)(2,1)S(1)} %slice.36), channel_id=1, source_target_pairs={{0,4},{1,5},{2,6},{3,7},{4,8},{5,9},{6,10},{7,11},{8,12},{9,13},{1... | collective-permute-start | bytes 82952
  221.5 10.9 %slice-start = ((s8[4718592]{0:T(1024)(128)(4,1)}), s8[4194304]{0:T(1024)(128)(4,1)S(1)}, s32[]{:S(2)}) async-start(s8[4718592]{0:T(1024)(128)(4,1)} %bitcast.46), calls=%async_computation.3 | async-start | bytes 8388608
  221.5 10.9 %slice-start.4 = ((s8[4718592]{0:T(1024)(128)(4,1)}), s8[4194304]{0:T(1024)(128)(4,1)S(1)}, s32[]{:S(2)}) async-start(s8[4718592]{0:T(1024)(128)(4,1)} %bitcast.50), calls=%async_computation.7 | async-start | bytes 8388608
  227.3 5.1 %slice-start.1 = ((s8[4718592]{0:T(1024)(128)(4,1)}), s8[524288]{0:T(1024)(128)(4,1)S(1)}, s32[]{:S(2)}) async-start(s8[4718592]{0:T(1024)(128)(4,1)} %bitcast.46), calls=%async_computation.4 | async-start | bytes 1048576
  227.3 5.1 %slice-start.5 = ((s8[4718592]{0:T(1024)(128)(4,1)}), s8[524288]{0:T(1024)(128)(4,1)S(1)}, s32[]{:S(2)}) async-start(s8[4718592]{0:T(1024)(128)(4,1)} %bitcast.50), calls=%async_computation.8 | async-start | bytes 1048576
  253.2 10.5 %copy-start.1 = (bf16[2,576,1152]{2,1,0:T(8,128)(2,1)S(1)}, bf16[2,576,1152]{2,1,0:T(8,128)(2,1)}, u32[]{:S(2)}) copy-start(bf16[2,576,1152]{2,1,0:T(8,128)(2,1)} %param.12) | copy-start | bytes 7962628
Sparse Core Ops, SparseCore 0:
  63.6 14.4 all-reduce.10
  80.5 21.5 all-reduce.6
  236.7 14.8 all-reduce.8
where the time goes:
time: 271 us; the launch traced here: 270 us
  blocking collectives  140 us (52%)
  matrix products  53 us (20%)
  other arithmetic  24.3 us (9%)
  waiting for transfers between devices  17.8 us (7%)
  between operations  14.6 us (5%)
  local copies, waits for them, and re-layouts  13.5 us (5%)
  starting transfers between devices  6.99 us (3%)
    unnamed x1, blocking collectives  49 us
    all_gather x1, blocking collectives, body(): normed = lax.all_gather(normed_local, 'feat', axis=1, tiled=True)  44.8 us
    all_gather x1, blocking collectives, body(): errors = lax.all_gather(errors_local, 'feat', axis=0, tiled=True)  43.6 us
    psum x1, waiting for transfers between devices, body(): preact = lax.psum(preact_part, 'mp')  17.4 us
    convert_element_type x1, other arithmetic, body(): grad_decoder = (loss_scale * jnp.stack([outer_product(active_first, error...  16.6 us
    dot_general x3, matrix products, outer_product(): lax.dot_general(weights_side, errors_side, (((0,), (0,)), ((), ())), pref...  15.9 us
    squeeze x1, local copies, waits for them, and re-layouts, body(): decoder[0]  11.3 us
    dot_general x1, matrix products, body(): jnp.einsum('ltd,lfd->tlf', normed, encoder, preferred_element_type=jnp.fl...  8.01 us
  transfers between devices with their start and end apart: 7, of which 2 were waited for; matrix products, arithmetic and copies ran while one was open for 14% of the time, Pallas kernels for 0%

commit v1 on v0

--- a/solution.py
+++ b/solution.py
@@ -19,7 +19,14 @@
     squares = lax.psum(jnp.sum(values * values, axis=2), "mp")
     inverse_rms = lax.rsqrt(squares / D + 1e-06)
     normed_local = (values * inverse_rms[:, :, None] * norm_gain[:, None, :]).astype(jnp.bfloat16)
-    normed = lax.all_gather(normed_local, "feat", axis=1, tiled=True)
+    size = lax.axis_size("feat")
+    hops = [(i, (i + 1) % size) for i in range(size)]
+    parts = [normed_local]
+    for far in range(1, size):
+        parts = [lax.ppermute(parts[0], "feat", hops), *parts]
+    full = jnp.concatenate(parts, axis=1)
+    shift = (lax.axis_index("feat") + 1) * parts[-1].shape[1]
+    normed = jnp.roll(full, shift, axis=1)
     tokens = normed.shape[1]
     local_rows = residual.shape[1]
     gate_part = jnp.einsum("ltd,ldh->lth", normed, gate_weight, preferred_element_type=jnp.float32)

time: 271 us -> 379 us (1.40)
  waiting for transfers between devices: 17.8 us -> 129 us
  blocking collectives: 140 us -> 95.2 us
  local copies, waits for them, and re-layouts: 13.5 us -> 49.9 us
    ppermute x0 -> x15, waiting for transfers between devices: none -> 111 us  [body(): parts = [lax.ppermute(parts[0], 'feat', hops), *parts]]
    all_gather x1 -> x0, blocking collectives: 44.8 us -> none  [body(): normed = lax.all_gather(normed_local, 'feat', axis=1, tiled=True)]
    concatenate x0 -> x1, local copies, waits for them, and re-layouts: none -> 27.4 us  [body(): normed = jnp.roll(full, shift, axis=1)]
    unnamed x31 -> x61, local copies, waits for them, and re-layouts: 2.02 us -> 11.2 us
  transfers between devices with their start and end apart: 7 -> 22, of which waited for: 2 -> 17; matrix products, arithmetic and copies ran while one was open for 14% -> 10% of each run, Pallas kernels for 0% -> 0%
where the time goes in v1:
time: 379 us; the launch traced here: 376 us
  waiting for transfers between devices  129 us (34%)
  blocking collectives  95.2 us (25%)
  matrix products  53.3 us (14%)
  local copies, waits for them, and re-layouts  49.9 us (13%)
  other arithmetic  24.3 us (6%)
  between operations  14.7 us (4%)
  starting transfers between devices  9.83 us (3%)
    ppermute x15, waiting for transfers between devices, body(): parts = [lax.ppermute(parts[0], 'feat', hops), *parts]  111 us
    unnamed x1, blocking collectives  49 us
    all_gather x1, blocking collectives, body(): errors = lax.all_gather(errors_local, 'feat', axis=0, tiled=True)  43.6 us
    concatenate x1, local copies, waits for them, and re-layouts, body(): normed = jnp.roll(full, shift, axis=1)  27.4 us
    psum x1, waiting for transfers between devices, body(): preact = lax.psum(preact_part, 'mp')  17.3 us
    convert_element_type x1, other arithmetic, body(): grad_decoder = (loss_scale * jnp.stack([outer_product(active_first, error...  16.6 us
    dot_general x3, matrix products, outer_product(): lax.dot_general(weights_side, errors_side, (((0,), (0,)), ((), ())), pref...  15.9 us
    squeeze x1, local copies, waits for them, and re-layouts, body(): decoder[0]  11.3 us
  transfers between devices with their start and end apart: 22, of which 17 were waited for; matrix products, arithmetic and copies ran while one was open for 10% of the time, Pallas kernels for 0%

profile of v1, /device:TPU:0, one launch (start us, length us, event | category | flops | bytes accessed | tf_op | source)
XLA Modules:
  0.0 376.1 jit_solution(5873283820091917898)
XLA Ops:
  15.1 5.9 %collective-permute-done = bf16[2,6,1152]{2,1,0:T(8,128)(2,1)S(1)} collective-permute-done((bf16[2,6,1152]{2,1,0:T(8,128)(2,1)S(1)}, bf16[2,6,1152]{2,1,0:T(8,128)(2,1)S(1)}, u32[]{:S(2)}, u32[]{:S(2)}) %collective-permute-start) | collective-permute-done | bytes 27680 | tf_op jit(solution)/shard_map/ppermute | solution.py:26
  21.6 7.6 %collective-permute-done.1 = bf16[2,6,1152]{2,1,0:T(8,128)(2,1)S(1)} collective-permute-done((bf16[2,6,1152]{2,1,0:T(8,128)(2,1)S(1)}, bf16[2,6,1152]{2,1,0:T(8,128)(2,1)S(1)}, u32[]{:S(2)}, u32[]{:S(2)}) %collective-permute-start.1) | collective-permute-done | bytes 27680 | tf_op jit(solution)/shard_map/ppermute | solution.py:26
  29.8 7.6 %collective-permute-done.2 = bf16[2,6,1152]{2,1,0:T(8,128)(2,1)S(1)} collective-permute-done((bf16[2,6,1152]{2,1,0:T(8,128)(2,1)S(1)}, bf16[2,6,1152]{2,1,0:T(8,128)(2,1)S(1)}, u32[]{:S(2)}, u32[]{:S(2)}) %collective-permute-start.2) | collective-permute-done | bytes 27680 | tf_op jit(solution)/shard_map/ppermute | solution.py:26
  38.0 7.6 %collective-permute-done.3 = bf16[2,6,1152]{2,1,0:T(8,128)(2,1)S(1)} collective-permute-done((bf16[2,6,1152]{2,1,0:T(8,128)(2,1)S(1)}, bf16[2,6,1152]{2,1,0:T(8,128)(2,1)S(1)}, u32[]{:S(2)}, u32[]{:S(2)}) %collective-permute-start.3) | collective-permute-done | bytes 27680 | tf_op jit(solution)/shard_map/ppermute | solution.py:26
  46.1 7.6 %collective-permute-done.4 = bf16[2,6,1152]{2,1,0:T(8,128)(2,1)S(1)} collective-permute-done((bf16[2,6,1152]{2,1,0:T(8,128)(2,1)S(1)}, bf16[2,6,1152]{2,1,0:T(8,128)(2,1)S(1)}, u32[]{:S(2)}, u32[]{:S(2)}) %collective-permute-start.4) | collective-permute-done | bytes 27680 | tf_op jit(solution)/shard_map/ppermute | solution.py:26
  54.3 7.6 %collective-permute-done.5 = bf16[2,6,1152]{2,1,0:T(8,128)(2,1)S(1)} collective-permute-done((bf16[2,6,1152]{2,1,0:T(8,128)(2,1)S(1)}, bf16[2,6,1152]{2,1,0:T(8,128)(2,1)S(1)}, u32[]{:S(2)}, u32[]{:S(2)}) %collective-permute-start.5) | collective-permute-done | bytes 27680 | tf_op jit(solution)/shard_map/ppermute | solution.py:26
  62.5 7.6 %collective-permute-done.6 = bf16[2,6,1152]{2,1,0:T(8,128)(2,1)S(1)} collective-permute-done((bf16[2,6,1152]{2,1,0:T(8,128)(2,1)S(1)}, bf16[2,6,1152]{2,1,0:T(8,128)(2,1)S(1)}, u32[]{:S(2)}, u32[]{:S(2)}) %collective-permute-start.6) | collective-permute-done | bytes 27680 | tf_op jit(solution)/shard_map/ppermute | solution.py:26
  70.6 7.6 %collective-permute-done.7 = bf16[2,6,1152]{2,1,0:T(8,128)(2,1)S(1)} collective-permute-done((bf16[2,6,1152]{2,1,0:T(8,128)(2,1)S(1)}, bf16[2,6,1152]{2,1,0:T(8,128)(2,1)S(1)}, u32[]{:S(2)}, u32[]{:S(2)}) %collective-permute-start.7) | collective-permute-done | bytes 27680 | tf_op jit(solution)/shard_map/ppermute | solution.py:26
  78.8 7.6 %collective-permute-done.8 = bf16[2,6,1152]{2,1,0:T(8,128)(2,1)S(1)} collective-permute-done((bf16[2,6,1152]{2,1,0:T(8,128)(2,1)S(1)}, bf16[2,6,1152]{2,1,0:T(8,128)(2,1)S(1)}, u32[]{:S(2)}, u32[]{:S(2)}) %collective-permute-start.8) | collective-permute-done | bytes 27680 | tf_op jit(solution)/shard_map/ppermute | solution.py:26
  87.0 7.6 %collective-permute-done.9 = bf16[2,6,1152]{2,1,0:T(8,128)(2,1)S(1)} collective-permute-done((bf16[2,6,1152]{2,1,0:T(8,128)(2,1)S(1)}, bf16[2,6,1152]{2,1,0:T(8,128)(2,1)S(1)}, u32[]{:S(2)}, u32[]{:S(2)}) %collective-permute-start.9) | collective-permute-done | bytes 27680 | tf_op jit(solution)/shard_map/ppermute | solution.py:26
  95.1 7.6 %collective-permute-done.10 = bf16[2,6,1152]{2,1,0:T(8,128)(2,1)S(1)} collective-permute-done((bf16[2,6,1152]{2,1,0:T(8,128)(2,1)S(1)}, bf16[2,6,1152]{2,1,0:T(8,128)(2,1)S(1)}, u32[]{:S(2)}, u32[]{:S(2)}) %collective-permute-start.10) | collective-permute-done | bytes 27680 | tf_op jit(solution)/shard_map/ppermute | solution.py:26
  103.3 7.6 %collective-permute-done.11 = bf16[2,6,1152]{2,1,0:T(8,128)(2,1)S(1)} collective-permute-done((bf16[2,6,1152]{2,1,0:T(8,128)(2,1)S(1)}, bf16[2,6,1152]{2,1,0:T(8,128)(2,1)S(1)}, u32[]{:S(2)}, u32[]{:S(2)}) %collective-permute-start.11) | collective-permute-done | bytes 27680 | tf_op jit(solution)/shard_map/ppermute | solution.py:26
  111.4 7.6 %collective-permute-done.12 = bf16[2,6,1152]{2,1,0:T(8,128)(2,1)S(1)} collective-permute-done((bf16[2,6,1152]{2,1,0:T(8,128)(2,1)S(1)}, bf16[2,6,1152]{2,1,0:T(8,128)(2,1)S(1)}, u32[]{:S(2)}, u32[]{:S(2)}) %collective-permute-start.12) | collective-permute-done | bytes 27680 | tf_op jit(solution)/shard_map/ppermute | solution.py:26
  119.6 7.6 %collective-permute-done.13 = bf16[2,6,1152]{2,1,0:T(8,128)(2,1)S(1)} collective-permute-done((bf16[2,6,1152]{2,1,0:T(8,128)(2,1)S(1)}, bf16[2,6,1152]{2,1,0:T(8,128)(2,1)S(1)}, u32[]{:S(2)}, u32[]{:S(2)}) %collective-permute-start.13) | collective-permute-done | bytes 27680 | tf_op jit(solution)/shard_map/ppermute | solution.py:26
  127.8 7.0 %collective-permute-done.14 = bf16[2,6,1152]{2,1,0:T(8,128)(2,1)} collective-permute-done((bf16[2,6,1152]{2,1,0:T(8,128)(2,1)S(1)}, bf16[2,6,1152]{2,1,0:T(8,128)(2,1)}, u32[]{:S(2)}, u32[]{:S(2)}) %collective-permute-start.14) | collective-permute-done | bytes 27680 | tf_op jit(solution)/shard_map/ppermute | solution.py:26
  134.8 27.4 %concatenate.15 = bf16[2,192,1152]{2,1,0:T(8,128)(2,1)S(1)} concatenate(bf16[2,6,1152]{2,1,0:T(8,128)(2,1)} %collective-permute-done.14, bf16[2,6,1152]{2,1,0:T(8,128)(2,1)} %copy-done.20, bf16[2,6,1152]{2,1,0:T(8,128)(2,1)} %copy-done.19, bf16[2,6,1152]{2,1,0:T(8,128)(2,1)} %copy-done.18, bf16[2,6,1152]{2,1,0:T(8,128)(2,1)} %copy-done.17, bf16[2,6,1152]{2,1,0:T(8,128)(2,1)} %copy-done.16, ...), dimensions={1} | concatenate | bytes 1769472 | tf_op jit(solution)/shard_map/jit(_roll_dynamic)/concatenate | solution.py:29
  162.2 3.8 convolution_convert_fusion.3
  165.9 3.4 convolution_convert_fusion.2
  169.4 8.0 %convolution_bitcast_fusion.4 = f32[96,2,2048]{2,0,1:T(8,128)} fusion(bf16[2,2048,1152]{2,1,0:T(8,128)(2,1)} %param.13, bf16[2,192,1152]{2,1,0:T(8,128)(2,1)S(1)} %concatenate.15, s32[]{:T(128)S(6)} %select_n.18), kind=kOutput, calls=%fused_computation.18 | convolution fusion | flops 905969664 | bytes 11452420 | tf_op jit(solution)/shard_map/ltd,lfd->tlf/dot_general | solution.py:39
  177.6 11.3 %slice_bitcast_fusion.2 = (bf16[2048,1152]{1,0:T(8,128)(2,1)}, bf16[2048,1152]{1,0:T(8,128)(2,1)}, bf16[2048,1152]{1,0:T(8,128)(2,1)}) fusion(bf16[3,2048,1152]{2,1,0:T(8,128)(2,1)} %param.15), kind=kLoop, calls=%fused_computation.16 | loop fusion | bytes 28311552 | tf_op jit(solution)/shard_map/squeeze | solution.py:50
  190.6 17.3 %all-reduce.7.cloned.1.call-done = f32[96,2,2048]{2,0,1:T(8,128)} async-done(((f32[96,2,2048]{2,0,1:T(8,128)}), f32[96,2,2048]{2,0,1:T(8,128)}) %all-reduce.7.cloned.1.call-update) | async-done | bytes 1572880 | tf_op jit(solution)/shard_map/psum | solution.py:40
  209.7 3.7 fusion.24
  216.5 49.0 %fusion = f32[8,2304]{1,0:T(8,128)S(1)} fusion(f32[96,2304]{1,0:T(8,128)S(1)} %maximum_subtract_fusion), kind=kCustom, calls=%all-reduce-scatter | all-reduce-scatter fusion | flops 294913 | bytes 958976
  274.6 43.6 %all-gather = bf16[16,6,2304]{2,1,0:T(8,128)(2,1)S(1)} all-gather(bf16[1,6,2304]{2,1,0:T(8,128)(2,1)S(1)} %fusion.41), channel_id=1, replica_groups=mesh['mp'=2,'feat'=16] {'feat'}, dimensions={0}, use_global_device_ids=true | all-gather | bytes 470016 | tf_op jit(solution)/shard_map/all_gather | solution.py:63
  318.4 3.9 %fusion.16 = bf16[96,1,2048]{2,0,1:T(8,128)(2,1)S(1)} fusion(bf16[96,2304]{1,0:T(8,128)(2,1)S(1)} %reshape.18, bf16[3,2048,1152]{2,1,0:T(8,128)(2,1)} %param.15), kind=kOutput, calls=%fused_computation.22 | convolution fusion | flops 453181440 | bytes 5332992 | tf_op jit(solution)/shard_map/dot_general | solution.py:70
  322.3 5.1 %convolution_bitcast_fusion.1 = f32[1,2048,1152]{2,1,0:T(8,128)} fusion(bf16[96,2,2048]{2,0,1:T(8,128)(2,1)S(1)} %maximum_convert_fusion, bf16[96,2304]{1,0:T(8,128)(2,1)S(1)} %reshape.18), kind=kOutput, calls=%fused_computation.12 | convolution fusion | flops 452984832 | bytes 10051584 | tf_op jit(solution)/shard_map/dot_general | solution.py:12
  327.4 5.8 %convolution_bitcast_fusion = f32[1,2048,1152]{2,1,0:T(8,128)} fusion(bf16[96,2,2048]{2,0,1:T(8,128)(2,1)S(1)} %maximum_convert_fusion, bf16[96,2304]{1,0:T(8,128)(2,1)S(1)} %reshape.18), kind=kOutput, calls=%fused_computation.11 | convolution fusion | flops 452984832 | bytes 10051584 | tf_op jit(solution)/shard_map/dot_general | solution.py:12
  333.2 5.1 %convolution_bitcast_fusion.2 = f32[1,2048,1152]{2,1,0:T(8,128)} fusion(bf16[96,2,2048]{2,0,1:T(8,128)(2,1)S(1)} %maximum_convert_fusion, bf16[96,2304]{1,0:T(8,128)(2,1)S(1)} %reshape.18), kind=kOutput, calls=%fused_computation.13 | convolution fusion | flops 452984832 | bytes 10051584 | tf_op jit(solution)/shard_map/dot_general | solution.py:12
  338.3 3.1 fusion.13
  342.4 16.6 %fusion.1 = bf16[3,2048,1152]{2,1,0:T(8,128)(2,1)} fusion(f32[1,2048,1152]{2,1,0:T(8,128)} %convolution_bitcast_fusion, f32[1,2048,1152]{2,1,0:T(8,128)} %convolution_bitcast_fusion.1, f32[1,2048,1152]{2,1,0:T(8,128)} %convolution_bitcast_fusion.2), kind=kLoop, calls=%fused_computation.1 | loop fusion | flops 28311552 | bytes 42467328 | tf_op jit(solution)/shard_map/convert_element_type | solution.py:94
  359.1 2.8 convert_reduce_fusion
  361.9 7.7 %convolution_convert_fusion = bf16[2,2048,1152]{2,1,0:T(8,128)(2,1)} fusion(bf16[2,192,1152]{2,1,0:T(8,128)(2,1)} %copy-done.3, s32[]{:T(128)S(6)} %select_n.18, bf16[96,2,2048]{2,0,1:T(8,128)(2,1)} %all-reduce.9.cloned.1.call-done, bf16[96,2,2048]{2,0,1:T(8,128)(2,1)S(1)} %maximum_convert_fusion), kind=kOutput, calls=%fused_computation.2 | convolution fusion | flops 913047552 | bytes 11452420 | tf_op jit(solution)/shard_map/tlf,ltd->lfd/dot_general | solution.py:79
  (108 shorter events, 32.7 us)
Async XLA Ops:
  7.2 181.7 %copy-start = (bf16[2,576,1152]{2,1,0:T(8,128)(2,1)S(1)}, bf16[2,576,1152]{2,1,0:T(8,128)(2,1)}, u32[]{:S(2)}) copy-start(bf16[2,576,1152]{2,1,0:T(8,128)(2,1)} %param.12) | copy-start | bytes 7962628
  7.2 181.7 %all-reduce.11.cloned.1.call-start = ((), (), s32[]{:S(2)}) async-start(), calls=%async_computation.2 | async-start | bytes 983040 | tf_op jit(solution)/shard_map/psum | solution.py:35
  12.3 8.7 %collective-permute-start = (bf16[2,6,1152]{2,1,0:T(8,128)(2,1)S(1)}, bf16[2,6,1152]{2,1,0:T(8,128)(2,1)S(1)}, u32[]{:S(2)}, u32[]{:S(2)}) collective-permute-start(bf16[2,6,1152]{2,1,0:T(8,128)(2,1)S(1)} %fusion.40), channel_id=1, source_target_pairs={{0,1},{1,2},{2,3},{3,4},{4,5},{5,6},{6,7},{7,8},{8,9},{9,10},{10,1... | collective-permute-start | bytes 82952 | tf_op jit(solution)/shard_map/ppermute | solution.py:26
  21.6 7.6 %collective-permute-start.1 = (bf16[2,6,1152]{2,1,0:T(8,128)(2,1)S(1)}, bf16[2,6,1152]{2,1,0:T(8,128)(2,1)S(1)}, u32[]{:S(2)}, u32[]{:S(2)}) collective-permute-start(bf16[2,6,1152]{2,1,0:T(8,128)(2,1)S(1)} %collective-permute-done), channel_id=1, source_target_pairs={{0,1},{1,2},{2,3},{3,4},{4,5},{5,6},{6,7},{7,8},{8,9},{9,10},{10,1... | collective-permute-start | bytes 82952 | tf_op jit(solution)/shard_map/ppermute | solution.py:26
  29.8 7.6 %collective-permute-start.2 = (bf16[2,6,1152]{2,1,0:T(8,128)(2,1)S(1)}, bf16[2,6,1152]{2,1,0:T(8,128)(2,1)S(1)}, u32[]{:S(2)}, u32[]{:S(2)}) collective-permute-start(bf16[2,6,1152]{2,1,0:T(8,128)(2,1)S(1)} %collective-permute-done.1), channel_id=1, source_target_pairs={{0,1},{1,2},{2,3},{3,4},{4,5},{5,6},{6,7},{7,8},{8,9},{9,10},{10,1... | collective-permute-start | bytes 82952 | tf_op jit(solution)/shard_map/ppermute | solution.py:26
  38.0 7.6 %collective-permute-start.3 = (bf16[2,6,1152]{2,1,0:T(8,128)(2,1)S(1)}, bf16[2,6,1152]{2,1,0:T(8,128)(2,1)S(1)}, u32[]{:S(2)}, u32[]{:S(2)}) collective-permute-start(bf16[2,6,1152]{2,1,0:T(8,128)(2,1)S(1)} %collective-permute-done.2), channel_id=1, source_target_pairs={{0,1},{1,2},{2,3},{3,4},{4,5},{5,6},{6,7},{7,8},{8,9},{9,10},{10,1... | collective-permute-start | bytes 82952 | tf_op jit(solution)/shard_map/ppermute | solution.py:26
  46.1 7.6 %collective-permute-start.4 = (bf16[2,6,1152]{2,1,0:T(8,128)(2,1)S(1)}, bf16[2,6,1152]{2,1,0:T(8,128)(2,1)S(1)}, u32[]{:S(2)}, u32[]{:S(2)}) collective-permute-start(bf16[2,6,1152]{2,1,0:T(8,128)(2,1)S(1)} %collective-permute-done.3), channel_id=1, source_target_pairs={{0,1},{1,2},{2,3},{3,4},{4,5},{5,6},{6,7},{7,8},{8,9},{9,10},{10,1... | collective-permute-start | bytes 82952 | tf_op jit(solution)/shard_map/ppermute | solution.py:26
  54.3 7.6 %collective-permute-start.5 = (bf16[2,6,1152]{2,1,0:T(8,128)(2,1)S(1)}, bf16[2,6,1152]{2,1,0:T(8,128)(2,1)S(1)}, u32[]{:S(2)}, u32[]{:S(2)}) collective-permute-start(bf16[2,6,1152]{2,1,0:T(8,128)(2,1)S(1)} %collective-permute-done.4), channel_id=1, source_target_pairs={{0,1},{1,2},{2,3},{3,4},{4,5},{5,6},{6,7},{7,8},{8,9},{9,10},{10,1... | collective-permute-start | bytes 82952 | tf_op jit(solution)/shard_map/ppermute | solution.py:26
  62.5 7.6 %collective-permute-start.6 = (bf16[2,6,1152]{2,1,0:T(8,128)(2,1)S(1)}, bf16[2,6,1152]{2,1,0:T(8,128)(2,1)S(1)}, u32[]{:S(2)}, u32[]{:S(2)}) collective-permute-start(bf16[2,6,1152]{2,1,0:T(8,128)(2,1)S(1)} %collective-permute-done.5), channel_id=1, source_target_pairs={{0,1},{1,2},{2,3},{3,4},{4,5},{5,6},{6,7},{7,8},{8,9},{9,10},{10,1... | collective-permute-start | bytes 82952 | tf_op jit(solution)/shard_map/ppermute | solution.py:26
  70.6 7.6 %collective-permute-start.7 = (bf16[2,6,1152]{2,1,0:T(8,128)(2,1)S(1)}, bf16[2,6,1152]{2,1,0:T(8,128)(2,1)S(1)}, u32[]{:S(2)}, u32[]{:S(2)}) collective-permute-start(bf16[2,6,1152]{2,1,0:T(8,128)(2,1)S(1)} %collective-permute-done.6), channel_id=1, source_target_pairs={{0,1},{1,2},{2,3},{3,4},{4,5},{5,6},{6,7},{7,8},{8,9},{9,10},{10,1... | collective-permute-start | bytes 82952 | tf_op jit(solution)/shard_map/ppermute | solution.py:26
  78.8 7.6 %collective-permute-start.8 = (bf16[2,6,1152]{2,1,0:T(8,128)(2,1)S(1)}, bf16[2,6,1152]{2,1,0:T(8,128)(2,1)S(1)}, u32[]{:S(2)}, u32[]{:S(2)}) collective-permute-start(bf16[2,6,1152]{2,1,0:T(8,128)(2,1)S(1)} %collective-permute-done.7), channel_id=1, source_target_pairs={{0,1},{1,2},{2,3},{3,4},{4,5},{5,6},{6,7},{7,8},{8,9},{9,10},{10,1... | collective-permute-start | bytes 82952 | tf_op jit(solution)/shard_map/ppermute | solution.py:26
  87.0 7.6 %collective-permute-start.9 = (bf16[2,6,1152]{2,1,0:T(8,128)(2,1)S(1)}, bf16[2,6,1152]{2,1,0:T(8,128)(2,1)S(1)}, u32[]{:S(2)}, u32[]{:S(2)}) collective-permute-start(bf16[2,6,1152]{2,1,0:T(8,128)(2,1)S(1)} %collective-permute-done.8), channel_id=1, source_target_pairs={{0,1},{1,2},{2,3},{3,4},{4,5},{5,6},{6,7},{7,8},{8,9},{9,10},{10,1... | collective-permute-start | bytes 82952 | tf_op jit(solution)/shard_map/ppermute | solution.py:26
  95.1 7.6 %collective-permute-start.10 = (bf16[2,6,1152]{2,1,0:T(8,128)(2,1)S(1)}, bf16[2,6,1152]{2,1,0:T(8,128)(2,1)S(1)}, u32[]{:S(2)}, u32[]{:S(2)}) collective-permute-start(bf16[2,6,1152]{2,1,0:T(8,128)(2,1)S(1)} %collective-permute-done.9), channel_id=1, source_target_pairs={{0,1},{1,2},{2,3},{3,4},{4,5},{5,6},{6,7},{7,8},{8,9},{9,10},{10,1... | collective-permute-start | bytes 82952 | tf_op jit(solution)/shard_map/ppermute | solution.py:26
  103.3 7.6 %collective-permute-start.11 = (bf16[2,6,1152]{2,1,0:T(8,128)(2,1)S(1)}, bf16[2,6,1152]{2,1,0:T(8,128)(2,1)S(1)}, u32[]{:S(2)}, u32[]{:S(2)}) collective-permute-start(bf16[2,6,1152]{2,1,0:T(8,128)(2,1)S(1)} %collective-permute-done.10), channel_id=1, source_target_pairs={{0,1},{1,2},{2,3},{3,4},{4,5},{5,6},{6,7},{7,8},{8,9},{9,10},{10,1... | collective-permute-start | bytes 82952 | tf_op jit(solution)/shard_map/ppermute | solution.py:26
  111.4 7.6 %collective-permute-start.12 = (bf16[2,6,1152]{2,1,0:T(8,128)(2,1)S(1)}, bf16[2,6,1152]{2,1,0:T(8,128)(2,1)S(1)}, u32[]{:S(2)}, u32[]{:S(2)}) collective-permute-start(bf16[2,6,1152]{2,1,0:T(8,128)(2,1)S(1)} %collective-permute-done.11), channel_id=1, source_target_pairs={{0,1},{1,2},{2,3},{3,4},{4,5},{5,6},{6,7},{7,8},{8,9},{9,10},{10,1... | collective-permute-start | bytes 82952 | tf_op jit(solution)/shard_map/ppermute | solution.py:26
  119.6 7.6 %collective-permute-start.13 = (bf16[2,6,1152]{2,1,0:T(8,128)(2,1)S(1)}, bf16[2,6,1152]{2,1,0:T(8,128)(2,1)S(1)}, u32[]{:S(2)}, u32[]{:S(2)}) collective-permute-start(bf16[2,6,1152]{2,1,0:T(8,128)(2,1)S(1)} %collective-permute-done.12), channel_id=1, source_target_pairs={{0,1},{1,2},{2,3},{3,4},{4,5},{5,6},{6,7},{7,8},{8,9},{9,10},{10,1... | collective-permute-start | bytes 82952 | tf_op jit(solution)/shard_map/ppermute | solution.py:26
  127.2 7.7 %collective-permute-start.14 = (bf16[2,6,1152]{2,1,0:T(8,128)(2,1)S(1)}, bf16[2,6,1152]{2,1,0:T(8,128)(2,1)}, u32[]{:S(2)}, u32[]{:S(2)}) collective-permute-start(bf16[2,6,1152]{2,1,0:T(8,128)(2,1)S(1)} %collective-permute-done.13), channel_id=1, source_target_pairs={{0,1},{1,2},{2,3},{3,4},{4,5},{5,6},{6,7},{7,8},{8,9},{9,10},{10,1... | collective-permute-start | bytes 82952 | tf_op jit(solution)/shard_map/ppermute | solution.py:26
  162.2 15.3 %copy-start.3 = (bf16[2,192,1152]{2,1,0:T(8,128)(2,1)}, bf16[2,192,1152]{2,1,0:T(8,128)(2,1)S(1)}, u32[]{:S(2)}) copy-start(bf16[2,192,1152]{2,1,0:T(8,128)(2,1)S(1)} %concatenate.15) | copy-start | bytes 2654212
  169.4 38.6 %all-reduce.7.cloned.1.call-start = ((), (), s32[]{:S(2)}) async-start(), calls=%async_computation | async-start | bytes 3145728 | tf_op jit(solution)/shard_map/psum | solution.py:40
  177.5 181.5 %all-reduce.9.cloned.1.call-start = ((), (), s32[]{:S(2)}) async-start(), calls=%async_computation.1 | async-start | bytes 1572864 | tf_op jit(solution)/shard_map/psum | solution.py:75
  188.9 19.1 %copy-start.6 = (f32[2,2048]{1,0:T(2,128)S(1)}, f32[2,2048]{1,0:T(2,128)}, u32[]{:S(2)}) copy-start(f32[2,2048]{1,0:T(2,128)} %param.14) | copy-start | bytes 49156
  208.0 5.5 %copy-start.2 = (f32[96,2,2048]{2,0,1:T(8,128)S(1)}, f32[96,2,2048]{2,0,1:T(8,128)}, u32[]{:S(2)}) copy-start(f32[96,2,2048]{2,0,1:T(8,128)} %all-reduce.7.cloned.1.call-done) | copy-start | bytes 4718596
  208.0 5.7 %slice-start.2 = ((s8[4718592]{0:T(1024)(128)(4,1)}), s8[4194304]{0:T(1024)(128)(4,1)S(1)}, s32[]{:S(2)}) async-start(s8[4718592]{0:T(1024)(128)(4,1)} %bitcast.48), calls=%async_computation.5 | async-start | bytes 8388608
  214.3 58.1 %copy-start.21 = (u32[32]{0:T(128)S(1)}, u32[32]{0:T(128)}, u32[]{:S(2)}) copy-start(u32[32]{0:T(128)} %constant.53) | copy-start | bytes 388
  265.5 8.5 %collective-permute-start.16 = (bf16[8,2304]{1,0:T(8,128)(2,1)S(1)}, bf16[8,2304]{1,0:T(8,128)(2,1)S(1)}, u32[]{:S(2)}, u32[]{:S(2)}) collective-permute-start(bf16[8,2304]{1,0:T(8,128)(2,1)S(1)} %convert.22), channel_id=1, source_target_pairs={{0,2},{1,3},{2,4},{3,5},{4,6},{5,7},{6,8},{7,9},{8,10},{9,11},{10,... | collective-permute-start | bytes 110600
  266.8 7.2 %collective-permute-start.17 = (bf16[8,2304]{1,0:T(8,128)(2,1)S(1)}, bf16[8,2304]{1,0:T(8,128)(2,1)S(1)}, u32[]{:S(2)}, u32[]{:S(2)}) collective-permute-start(bf16[8,2304]{1,0:T(8,128)(2,1)S(1)} %convert.22), channel_id=1, source_target_pairs={{0,3},{1,4},{2,5},{3,6},{4,7},{5,8},{6,9},{7,10},{8,11},{9,12},{10... | collective-permute-start | bytes 110600
  268.1 5.9 %collective-permute-start.15 = (bf16[8,2304]{1,0:T(8,128)(2,1)S(1)}, bf16[8,2304]{1,0:T(8,128)(2,1)S(1)}, u32[]{:S(2)}, u32[]{:S(2)}) collective-permute-start(bf16[8,2304]{1,0:T(8,128)(2,1)S(1)} %convert.22), channel_id=1, source_target_pairs={{0,1},{1,2},{2,3},{3,4},{4,5},{5,6},{6,7},{7,8},{8,9},{9,10},{10,1... | collective-permute-start | bytes 110600
  270.0 4.0 %collective-permute-start.18 = (bf16[6,2304]{1,0:T(8,128)(2,1)S(1)}, bf16[6,2304]{1,0:T(8,128)(2,1)S(1)}, u32[]{:S(2)}, u32[]{:S(2)}) collective-permute-start(bf16[6,2304]{1,0:T(8,128)(2,1)S(1)} %slice.36), channel_id=1, source_target_pairs={{0,4},{1,5},{2,6},{3,7},{4,8},{5,9},{6,10},{7,11},{8,12},{9,13},{1... | collective-permute-start | bytes 82952
  327.4 10.9 %slice-start = ((s8[4718592]{0:T(1024)(128)(4,1)}), s8[4194304]{0:T(1024)(128)(4,1)S(1)}, s32[]{:S(2)}) async-start(s8[4718592]{0:T(1024)(128)(4,1)} %bitcast.46), calls=%async_computation.3 | async-start | bytes 8388608
  327.4 10.9 %slice-start.4 = ((s8[4718592]{0:T(1024)(128)(4,1)}), s8[4194304]{0:T(1024)(128)(4,1)S(1)}, s32[]{:S(2)}) async-start(s8[4718592]{0:T(1024)(128)(4,1)} %bitcast.50), calls=%async_computation.7 | async-start | bytes 8388608
  333.1 5.1 %slice-start.5 = ((s8[4718592]{0:T(1024)(128)(4,1)}), s8[524288]{0:T(1024)(128)(4,1)S(1)}, s32[]{:S(2)}) async-start(s8[4718592]{0:T(1024)(128)(4,1)} %bitcast.50), calls=%async_computation.8 | async-start | bytes 1048576
  359.1 10.5 %copy-start.1 = (bf16[2,576,1152]{2,1,0:T(8,128)(2,1)S(1)}, bf16[2,576,1152]{2,1,0:T(8,128)(2,1)}, u32[]{:S(2)}) copy-start(bf16[2,576,1152]{2,1,0:T(8,128)(2,1)} %param.12) | copy-start | bytes 7962628
  (18 other events, 22.8 us)
Sparse Core Ops, SparseCore 0:
  169.5 14.4 all-reduce.10
  186.4 21.5 all-reduce.6
  342.5 14.8 all-reduce.8
